TPU v7x, 32 devices: a whole 2x2x4 slice. The times are simulated.
32 devices in a mesh: parts: 2 (over y), slab: 4 (over z), blk: 2 (over x), head: 2 (over core).
Axes of the slice: x: 2, y: 2, z: 4, core: 2. Of those that a mesh axis runs over, the one named last changes fastest.
Arguments:
- features: bfloat16 [4096, 512], P(('parts', 'slab', 'blk')), parts along dimension 0, may hold values from -16 to 16
- cotangent: bfloat16 [4096, 512], P(('parts', 'slab', 'blk')), parts along dimension 0, may hold values from -6 to 6
- w_query: bfloat16 [512, 512], P(None, 'head'), may hold values from -0.25 to 0.25
- w_key: bfloat16 [512, 512], P(None, 'head'), may hold values from -0.25 to 0.25
- w_value: bfloat16 [512, 512], P(None, 'head'), may hold values from -0.25 to 0.25
- w_out: bfloat16 [512, 512], P('head'), may hold values from -0.25 to 0.25
- adjacency: int32 [32, 3], P(('parts', 'slab', 'blk')), parts along dimension 0, may hold values from 0 to 1, as said below
- partner: int32 [3, 32], P(None, ('parts', 'slab', 'blk')), parts along dimension 1, may hold values from 0 to 15, as said below
- node_order: int32 [4096], P(('parts', 'slab', 'blk')), parts along dimension 0, may hold values from 0 to 255, as said below
Outputs:
- grad_input: bfloat16 [4096, 512], P(('parts', 'slab', 'blk'), 'head'), parts along dimension 0
There are 2 independent parts, one for each index of `parts`. A program takes and returns all parts, laid end to end along the dimension named above; an argument that names none is the same for every part. Nothing has to cross between parts.
Inputs may be any that keep to these rules, and one draw needn't show every extreme that they name: `adjacency`: column 1 (the block itself) is always 1. partner[m, g] is the block at the same position among its device's 2 blocks, on the device of the same blk index in another slab; partner[m, partner[m, g]] = g. Of the 3 * 2 (matching, block) pairs of one device, at most 2 have their partner in one slab, and on every device exactly 2 do for some slab. `node_order`: within each device's 2 * 128 positions, a permutation of the device's rows.
All inputs are finite; a program needn't handle non-finite values.
Results may differ from a plain program's by a relative error of at most 0.013.
The roundings to bfloat16 on the way count: a program that leaves them out, or rounds other values in their place, can miss the bound.
Values may be sent and summed in bfloat16 or wider, within the bound.
A program may use at most 64 MiB of HBM per device.

v0:
```python
import jax
import jax.numpy as jnp
from jax import lax
from jax.sharding import PartitionSpec as P

HEAD_DIM = 64


def padded_2(shard, sides, width):
    for axis, dim in sides:
        count, length = (lax.axis_size(axis), shard.shape[dim])
        up = [(i, (i + 1) % count) for i in range(count)]
        down = [(j, i) for i, j in up]
        last = lax.slice_in_dim(shard, length - width, length, axis=dim)
        first = lax.slice_in_dim(shard, 0, width, axis=dim)
        before = lax.ppermute(last, axis, up)
        after = lax.ppermute(first, axis, down)
        shard = jnp.concatenate([before, shard, after], axis=dim)
    return shard


def from_behind(value, axis, steps):
    count = lax.axis_size(axis)
    pairs = [(source, (source + steps) % count) for source in range(count)]
    return lax.ppermute(value, axis, pairs)


def attend(queries, grad_rows, key_rows, values, switch, score_scale):
    block_len = queries.shape[1]
    scores = (
        jnp.einsum("gqhd,gkhd->ghqk", queries, key_rows, preferred_element_type=jnp.float32)
        * score_scale
    )
    keys_on = jnp.repeat(switch, block_len, axis=1)
    scores = jnp.where(keys_on[:, None, None, :], scores, -jnp.inf)
    row_peak = jnp.max(scores, axis=-1, keepdims=True)
    row_total = jnp.log(jnp.sum(jnp.exp(scores - row_peak), axis=-1, keepdims=True)) + row_peak
    attention = jnp.exp(scores - row_total)
    attention_low = attention.astype(jnp.bfloat16)
    mixed_rows = jnp.einsum(
        "ghqk,gkhd->gqhd", attention_low, values, preferred_element_type=jnp.float32
    )
    row_dot = jnp.transpose(jnp.sum(grad_rows.astype(jnp.float32) * mixed_rows, axis=-1), (0, 2, 1))
    grad_attention = jnp.einsum(
        "gqhd,gkhd->ghqk", grad_rows, values, preferred_element_type=jnp.float32
    )
    grad_scores = (attention * (grad_attention - row_dot[..., None])).astype(jnp.bfloat16)
    grad_query = score_scale * jnp.einsum(
        "ghqk,gkhd->gqhd", grad_scores, key_rows, preferred_element_type=jnp.float32
    )
    grad_key = score_scale * jnp.einsum(
        "ghqk,gqhd->gkhd", grad_scores, queries, preferred_element_type=jnp.float32
    )
    grad_value = jnp.einsum(
        "ghqk,gqhd->gkhd", attention_low, grad_rows, preferred_element_type=jnp.float32
    )
    return (grad_query, grad_key, grad_value, row_total[..., 0], row_dot)


def to_slots(stacked, slot_block, block_count):
    blocked = stacked.reshape((stacked.shape[0], block_count, -1) + stacked.shape[2:])
    padded = jnp.concatenate([blocked, jnp.zeros_like(blocked[:, :1])], axis=1)
    return jnp.take(padded, slot_block, axis=1)


def body(features, cotangent, w_query, w_key, w_value, w_out, adjacency, partner, node_order):
    rows_dev = features.shape[0]
    block_count = adjacency.shape[0]
    block_len = rows_dev // block_count
    feat_width = w_query.shape[1]
    head_count = feat_width // HEAD_DIM
    score_scale = HEAD_DIM ** (-0.5)
    slab_count = lax.axis_size("slab")
    cycle_len = lax.axis_size("blk") * block_count
    capacity = max(1, (3 * block_count + slab_count - 2) // (slab_count - 1))
    slot_count = slab_count * capacity
    item_count = 3 * block_count
    inputs = jnp.take(features, node_order, axis=0)
    upstream = jnp.take(cotangent, node_order, axis=0)
    query_rows = jnp.dot(inputs, w_query, preferred_element_type=jnp.float32).astype(jnp.bfloat16)
    key_rows = jnp.dot(inputs, w_key, preferred_element_type=jnp.float32).astype(jnp.bfloat16)
    value_rows = jnp.dot(inputs, w_value, preferred_element_type=jnp.float32).astype(jnp.bfloat16)
    contract = (((1,), (1,)), ((), ()))
    grad_mix = lax.dot_general(
        upstream, w_out, contract, preferred_element_type=jnp.float32
    ).astype(jnp.bfloat16)
    pair_rows = jnp.stack([key_rows, value_rows])
    item_dest = (partner // cycle_len).reshape(-1)
    order_ids = jnp.arange(item_count, dtype=jnp.int32)
    earlier = order_ids[None, :] < order_ids[:, None]
    same_dest = item_dest[None, :] == item_dest[:, None]
    item_rank = jnp.sum((earlier & same_dest).astype(jnp.int32), axis=1)
    item_slot = item_dest * capacity + item_rank
    slot_ids = jnp.arange(slot_count, dtype=jnp.int32)
    slot_hit = (item_slot[None, :] == slot_ids[:, None]).astype(jnp.int32)
    slot_used = jnp.sum(slot_hit, axis=1)
    slot_item = jnp.sum(slot_hit * order_ids[None, :], axis=1) + (1 - slot_used) * item_count
    slot_block = jnp.where(slot_used > 0, slot_item % block_count, block_count)
    widened = padded_2(pair_rows, (("blk", 1),), block_len)
    widened = widened.reshape(2, block_count + 2, block_len, feat_width)
    near_rows = jnp.stack(
        [widened[:, offset : offset + block_count] for offset in range(3)], axis=2
    )
    sent_slots = to_slots(pair_rows, slot_block, block_count)
    arrived = lax.all_to_all(sent_slots, "slab", split_axis=1, concat_axis=1, tiled=True)
    far_rows = jnp.take(arrived, item_slot, axis=1)
    far_rows = far_rows.reshape(2, 3, block_count, block_len, feat_width)
    far_rows = jnp.transpose(far_rows, (0, 2, 1, 3, 4))
    gathered = jnp.concatenate([near_rows, far_rows], axis=2)
    gathered = gathered.reshape(2, block_count, 6 * block_len, head_count, HEAD_DIM)
    switch = jnp.concatenate([adjacency > 0, jnp.ones((block_count, 3), dtype=bool)], axis=1)
    query_blocks = query_rows.reshape(block_count, block_len, head_count, HEAD_DIM)
    grad_blocks = grad_mix.reshape(block_count, block_len, head_count, HEAD_DIM)

    def halves(source):
        return source.reshape((2, block_count // 2) + source.shape[1:])

    def visit_half(pieces):
        return attend(pieces[0], pieces[1], pieces[2], pieces[3], pieces[4], score_scale)

    results = lax.map(
        visit_half,
        (
            halves(query_blocks),
            halves(grad_blocks),
            halves(gathered[0]),
            halves(gathered[1]),
            halves(switch),
        ),
    )
    merged = [output.reshape((block_count,) + output.shape[2:]) for output in results]
    grad_query, grad_key, grad_value, row_total, row_dot = merged
    key_grads = jnp.stack([grad_key, grad_value]).reshape(2, block_count, -1, block_len, feat_width)
    extended = jnp.zeros((2, block_count + 2, block_len, feat_width), jnp.float32)
    for offset in range(3):
        extended = extended.at[:, offset : offset + block_count].add(key_grads[:, :, offset])
    from_right = from_behind(extended[:, :1].astype(jnp.bfloat16), "blk", -1).astype(jnp.float32)
    from_left = from_behind(extended[:, block_count + 1 :].astype(jnp.bfloat16), "blk", 1).astype(
        jnp.float32
    )
    own_grads = extended[:, 1 : block_count + 1]
    own_grads = own_grads.at[:, block_count - 1 :].add(from_right)
    own_grads = own_grads.at[:, :1].add(from_left)
    far_terms = jnp.transpose(key_grads[:, :, 3:], (0, 2, 1, 3, 4)).reshape(
        2, item_count, block_len, feat_width
    )
    padded = jnp.concatenate([far_terms, jnp.zeros_like(far_terms[:, :1])], axis=1)
    outgoing = jnp.take(padded, slot_item, axis=1)
    returned = lax.all_to_all(
        outgoing.astype(jnp.bfloat16), "slab", split_axis=1, concat_axis=1, tiled=True
    ).astype(outgoing.dtype)
    returned_terms = jnp.take(returned, item_slot, axis=1).reshape(
        2, 3, block_count, block_len, feat_width
    )
    own_grads = own_grads + jnp.sum(returned_terms, axis=1)
    grad_low = own_grads.reshape(2, rows_dev, feat_width).astype(jnp.bfloat16)
    query_low = grad_query.reshape(rows_dev, feat_width).astype(jnp.bfloat16)
    partial_sum = lax.dot_general(query_low, w_query, contract, preferred_element_type=jnp.float32)
    partial_sum = partial_sum + lax.dot_general(
        grad_low[0], w_key, contract, preferred_element_type=jnp.float32
    )
    partial_sum = partial_sum + lax.dot_general(
        grad_low[1], w_value, contract, preferred_element_type=jnp.float32
    )
    placed = jnp.zeros_like(partial_sum).at[node_order].set(partial_sum)
    head_share = lax.psum_scatter(
        placed.astype(jnp.bfloat16), "head", scatter_dimension=1, tiled=True
    )
    return head_share


def solution(mesh):
    in_specs = (
        P(("parts", "slab", "blk"), None),
        P(("parts", "slab", "blk"), None),
        P(None, "head"),
        P(None, "head"),
        P(None, "head"),
        P("head", None),
        P(("parts", "slab", "blk"), None),
        P(None, ("parts", "slab", "blk")),
        P(("parts", "slab", "blk")),
    )
    out_specs = P(("parts", "slab", "blk"), "head")
    return jax.shard_map(body, mesh=mesh, in_specs=in_specs, out_specs=out_specs, check_vma=False)
```

profile of v0, /device:TPU:0, one launch (start us, length us, event | category | flops | bytes accessed | tf_op | source)
XLA Modules:
  0.0 128.6 jit_solution(15643832790657309337)
XLA Ops:
  8.0 0.8 copy.68
  9.7 2.2 %gather_fusion.4 = bf16[256,512]{1,0:T(8,128)(2,1)S(1)} fusion(bf16[256,512]{1,0:T(8,128)(2,1)} %param.23, s32[1024]{0:T(1024)S(1)} %pad_clamp_fusion.3), kind=kCustom, calls=%fused_computation.clone | custom fusion | bytes 525312 | tf_op jit(solution)/shard_map/jit(_take)/gather | solution.py:78
  13.2 1.1 select_bitcast_fusion
  14.3 6.5 %all-to-all-start = ((bf16[2,8,128,256]{3,2,0,1:T(8,128)(2,1)}), bf16[2,8,128,256]{3,2,0,1:T(8,128)(2,1)S(1)}, u32[]{:S(2)}, u32[]{:S(2)}) async-start(bf16[2,8,128,256]{3,2,0,1:T(8,128)(2,1)} %select_bitcast_fusion), calls=%async_computation | async-start | bytes 2097152 | tf_op jit(solution)/shard_map/all_to_all | solution.py:105
  20.8 1.6 %collective-permute-start = (bf16[2,128,256]{2,1,0:T(8,128)(2,1)S(1)}, bf16[2,128,256]{2,1,0:T(8,128)(2,1)S(1)}, u32[]{:S(2)}, u32[]{:S(2)}) collective-permute-start(bf16[2,128,256]{2,1,0:T(8,128)(2,1)S(1)} %get-tuple-element.185), channel_id=1, source_target_pairs={{0,2},{2,0},{1,3},{3,1},{4,6},{6,4},{5,7},{7,5},{8,10},{10,8},{9,1... | collective-permute-start | bytes 393224 | tf_op jit(solution)/shard_map/ppermute | solution.py:16
  23.1 1.2 gather_fusion.5
  24.6 1.2 convolution_convert_fusion
  27.2 1.4 %collective-permute-done.1 = bf16[2,128,256]{2,1,0:T(8,128)(2,1)S(1)} collective-permute-done((bf16[2,128,256]{2,1,0:T(8,128)(2,1)S(1)}, bf16[2,128,256]{2,1,0:T(8,128)(2,1)S(1)}, u32[]{:S(2)}, u32[]{:S(2)}) %collective-permute-start.1) | collective-permute-done | bytes 131104 | tf_op jit(solution)/shard_map/ppermute | solution.py:17
  28.8 17.8 %all-to-all-done = bf16[2,8,128,256]{3,2,0,1:T(8,128)(2,1)S(1)} async-done(((bf16[2,8,128,256]{3,2,0,1:T(8,128)(2,1)}), bf16[2,8,128,256]{3,2,0,1:T(8,128)(2,1)S(1)}, u32[]{:S(2)}, u32[]{:S(2)}) %all-to-all-start) | async-done | bytes 1048608 | tf_op jit(solution)/shard_map/all_to_all | solution.py:105
  47.6 0.8 copy.75
  48.4 0.9 reshape_squeeze.6
  50.1 0.9 reshape_squeeze.7
  51.0 10.3 %while.19 = (s32[]{:T(128)}, bf16[2,1,128,4,64]{2,4,3,1,0:T(8,128)(2,1)S(1)}, f32[2,1,768,4,64]{2,4,3,1,0:T(8,128)}, f32[2,1,768,4,64]{2,4,3,1,0:T(8,128)}, bf16...) while((s32[]{:T(128)}, ...), condition=%wide.region_7.9_spmd, body=%wide.region_3.0_spmd.sunk | while | flops 307428352 | bytes 26441652 | solution.py:121
  54.6 1.2 fusion.105
  59.7 1.2 fusion.105
  61.9 2.7 %stack.40 = f32[1,2,6,128,256]{3,2,4,1,0:T(8,128)} reshape(f32[2,1,768,4,64]{2,4,3,1,0:T(8,128)} %get-tuple-element.116) | data formatting | bytes 3145728 | tf_op jit(solution)/shard_map/stack | solution.py:133
  64.6 1.9 %copy.85 = f32[1,2,6,128,256]{4,3,1,0,2:T(8,128)S(1)} copy(f32[1,2,6,128,256]{3,2,4,1,0:T(8,128)} %stack.40) | data formatting | bytes 3145728 | tf_op jit(solution)/shard_map/stack | solution.py:133
  66.6 1.6 %stack.41 = f32[1,2,6,128,256]{3,2,4,1,0:T(8,128)} reshape(f32[2,1,768,4,64]{2,4,3,1,0:T(8,128)S(1)} %copy-done.4) | data formatting | bytes 3145728 | tf_op jit(solution)/shard_map/stack | solution.py:133
  68.2 1.8 %copy.86 = f32[1,2,6,128,256]{4,3,1,0,2:T(8,128)S(1)} copy(f32[1,2,6,128,256]{3,2,4,1,0:T(8,128)} %stack.41) | data formatting | bytes 3145728 | tf_op jit(solution)/shard_map/stack | solution.py:133
  70.2 1.1 concatenate.31
  71.3 2.8 %gather_fusion.2 = bf16[8,2,128,256]{3,2,1,0:T(8,128)(2,1)} fusion(bf16[2,7,128,256]{3,2,1,0:T(8,128)(2,1)} %concatenate.31, s32[1024]{0:T(1024)S(1)} %get-tuple-element.191), kind=kCustom, calls=%fused_computation.4 | custom fusion | bytes 2097184 | tf_op jit(solution)/shard_map/jit(_take)/gather | solution.py:148
  74.1 2.6 %fusion.34 = bf16[2,8,128,256]{3,2,0,1:T(8,128)(2,1)} fusion(bf16[8,2,128,256]{3,2,1,0:T(8,128)(2,1)} %gather_fusion.2, pred[8]{0:T(512)(128)(4,1)S(1)} %copy-done.11), kind=kLoop, calls=%fused_computation.60 | loop fusion | flops 524288 | bytes 2097160 | tf_op jit(solution)/shard_map/convert_element_type | solution.py:150
  76.7 4.3 %all-to-all-start.1 = ((bf16[2,8,128,256]{3,2,0,1:T(8,128)(2,1)}), bf16[2,8,128,256]{3,2,0,1:T(8,128)(2,1)}, u32[]{:S(2)}, u32[]{:S(2)}) async-start(bf16[2,8,128,256]{3,2,0,1:T(8,128)(2,1)} %fusion.34), calls=%async_computation.1 | async-start | bytes 2097152 | tf_op jit(solution)/shard_map/all_to_all | solution.py:149
  81.6 1.6 %collective-permute-start.2 = (bf16[2,1,128,256]{3,2,1,0:T(8,128)(2,1)S(1)}, bf16[2,1,128,256]{3,2,1,0:T(8,128)(2,1)S(1)}, u32[]{:S(2)}, u32[]{:S(2)}) collective-permute-start(bf16[2,1,128,256]{3,2,1,0:T(8,128)(2,1)S(1)} %slice.266), channel_id=1, source_target_pairs={{0,2},{2,0},{1,3},{3,1},{4,6},{6,4},{5,7},{7,5},{8,10},{10,8},{9,1... | collective-permute-start | bytes 393224 | tf_op jit(solution)/shard_map/ppermute | solution.py:25
  84.1 3.4 %collective-permute-done.2 = bf16[2,1,128,256]{3,2,1,0:T(8,128)(2,1)S(1)} collective-permute-done((bf16[2,1,128,256]{3,2,1,0:T(8,128)(2,1)S(1)}, bf16[2,1,128,256]{3,2,1,0:T(8,128)(2,1)S(1)}, u32[]{:S(2)}, u32[]{:S(2)}) %collective-permute-start.2) | collective-permute-done | bytes 131104 | tf_op jit(solution)/shard_map/ppermute | solution.py:25
  87.6 1.4 %collective-permute-done.3 = bf16[2,1,128,256]{3,2,1,0:T(8,128)(2,1)S(1)} collective-permute-done((bf16[2,1,128,256]{3,2,1,0:T(8,128)(2,1)S(1)}, bf16[2,1,128,256]{3,2,1,0:T(8,128)(2,1)S(1)}, u32[]{:S(2)}, u32[]{:S(2)}) %collective-permute-start.3) | collective-permute-done | bytes 131104 | tf_op jit(solution)/shard_map/ppermute | solution.py:25
  89.0 17.2 %all-to-all-done.1 = bf16[2,8,128,256]{3,2,0,1:T(8,128)(2,1)} async-done(((bf16[2,8,128,256]{3,2,0,1:T(8,128)(2,1)}), bf16[2,8,128,256]{3,2,0,1:T(8,128)(2,1)}, u32[]{:S(2)}, u32[]{:S(2)}) %all-to-all-start.1) | async-done | bytes 1048608 | tf_op jit(solution)/shard_map/all_to_all | solution.py:149
  106.2 1.4 %convert_element_type.78 = f32[2,8,128,256]{3,2,0,1:T(8,128)S(1)} convert(bf16[2,8,128,256]{3,2,0,1:T(8,128)(2,1)} %all-to-all-done.1) | non-fusion elementwise | flops 524288 | bytes 3145728 | tf_op jit(solution)/shard_map/convert_element_type | solution.py:151
  107.7 1.8 %gather_fusion.3 = f32[6,2,128,256]{3,2,1,0:T(8,128)} fusion(f32[2,8,128,256]{3,2,0,1:T(8,128)S(1)} %convert_element_type.78, s32[1024]{0:T(1024)S(1)} %pad_clamp_fusion.1), kind=kCustom, calls=%fused_computation.5 | custom fusion | bytes 3145752 | tf_op jit(solution)/shard_map/jit(_take)/gather | solution.py:152
  109.4 1.6 %copy.88 = f32[2,6,128,256]{3,2,1,0:T(8,128)S(1)} copy(f32[2,6,128,256]{3,2,0,1:T(8,128)} %bitcast.204) | data formatting | bytes 3145728 | tf_op jit(solution)/shard_map/jit(_take)/gather | solution.py:152
  112.5 1.6 %scatter_custom_fusion = f32[256,512]{1,0:T(8,128)S(1)} fusion(s32[256]{0:T(256)S(1)} %compare_select_fusion.1, f32[256,512]{1,0:T(8,128)S(1)} %convolution_add_fusion, f32[]{:T(128)} %constant.251.clone.1), kind=kCustom, calls=%fused_computation.87 | custom fusion | bytes 524292 | tf_op jit(solution)/shard_map/scatter | solution.py:165
  114.9 6.9 %reduce-scatter.2.cloned.1.call-done = bf16[256,256]{1,0:T(8,128)(2,1)} async-done(((bf16[256,512]{1,0:T(8,128)(2,1)}), bf16[256,256]{1,0:T(8,128)(2,1)}) %reduce-scatter.2.cloned.1.call-update) | async-done | bytes 131088 | tf_op jit(solution)/shard_map/reduce_scatter | solution.py:166
  (112 shorter events, 20.6 us)
Async XLA Ops:
  6.5 17.8 %copy-start = (bf16[512,256]{1,0:T(8,128)(2,1)S(1)}, bf16[512,256]{1,0:T(8,128)(2,1)}, u32[]{:S(2)}) copy-start(bf16[512,256]{1,0:T(8,128)(2,1)} %param.25) | copy-start | bytes 786436
  6.5 5.4 %copy-start.5 = (bf16[512,256]{1,0:T(8,128)(2,1)S(1)}, bf16[512,256]{1,0:T(8,128)(2,1)}, u32[]{:S(2)}) copy-start(bf16[512,256]{1,0:T(8,128)(2,1)} %param.26) | copy-start | bytes 786436
  9.7 2.5 %copy-start.7 = (bf16[512,256]{1,0:T(8,128)(2,1)S(1)}, bf16[512,256]{1,0:T(8,128)(2,1)}, u32[]{:S(2)}) copy-start(bf16[512,256]{1,0:T(8,128)(2,1)} %param.27) | copy-start | bytes 786436
  14.3 8.7 %copy-start.1 = (bf16[256,512]{1,0:T(8,128)(2,1)S(1)}, bf16[256,512]{1,0:T(8,128)(2,1)}, u32[]{:S(2)}) copy-start(bf16[256,512]{1,0:T(8,128)(2,1)} %param.24) | copy-start | bytes 786436
  14.3 32.2 %all-to-all-start = ((bf16[2,8,128,256]{3,2,0,1:T(8,128)(2,1)}), bf16[2,8,128,256]{3,2,0,1:T(8,128)(2,1)S(1)}, u32[]{:S(2)}, u32[]{:S(2)}) async-start(bf16[2,8,128,256]{3,2,0,1:T(8,128)(2,1)} %select_bitcast_fusion), calls=%async_computation | async-start | bytes 2097152 | tf_op jit(solution)/shard_map/all_to_all | solution.py:105
  20.8 3.4 %copy-start.12 = (s32[2,3]{1,0:T(2,128)S(1)}, s32[2,3]{1,0:T(2,128)}, u32[]{:S(2)}) copy-start(s32[2,3]{1,0:T(2,128)} %param.29) | copy-start | bytes 76
  20.8 6.4 %collective-permute-start = (bf16[2,128,256]{2,1,0:T(8,128)(2,1)S(1)}, bf16[2,128,256]{2,1,0:T(8,128)(2,1)S(1)}, u32[]{:S(2)}, u32[]{:S(2)}) collective-permute-start(bf16[2,128,256]{2,1,0:T(8,128)(2,1)S(1)} %get-tuple-element.185), channel_id=1, source_target_pairs={{0,2},{2,0},{1,3},{3,1},{4,6},{6,4},{5,7},{7,5},{8,10},{10,8},{9,1... | collective-permute-start | bytes 393224 | tf_op jit(solution)/shard_map/ppermute | solution.py:16
  22.4 6.3 %collective-permute-start.1 = (bf16[2,128,256]{2,1,0:T(8,128)(2,1)S(1)}, bf16[2,128,256]{2,1,0:T(8,128)(2,1)S(1)}, u32[]{:S(2)}, u32[]{:S(2)}) collective-permute-start(bf16[2,128,256]{2,1,0:T(8,128)(2,1)S(1)} %get-tuple-element.186), channel_id=1, source_target_pairs={{2,0},{0,2},{3,1},{1,3},{6,4},{4,6},{7,5},{5,7},{10,8},{8,10},{11,... | collective-permute-start | bytes 393224 | tf_op jit(solution)/shard_map/ppermute | solution.py:17
  51.1 1.4 %copy-start.2 = (f32[2,1,768,4,64]{2,4,3,1,0:T(8,128)S(1)}, f32[2,1,768,4,64]{2,4,3,1,0:T(8,128)}, u32[]{:S(2)}) copy-start(f32[2,1,768,4,64]{2,4,3,1,0:T(8,128)} %get-tuple-element.265) | copy-start | bytes 4718596 | tf_op jit(solution)/shard_map/while
  52.9 1.1 copy-start.3
  56.2 1.4 %copy-start.2 = (f32[2,1,768,4,64]{2,4,3,1,0:T(8,128)S(1)}, f32[2,1,768,4,64]{2,4,3,1,0:T(8,128)}, u32[]{:S(2)}) copy-start(f32[2,1,768,4,64]{2,4,3,1,0:T(8,128)} %get-tuple-element.265) | copy-start | bytes 4718596 | tf_op jit(solution)/shard_map/while
  58.1 1.1 copy-start.3
  61.3 0.7 copy-start.9
  64.6 2.0 %copy-start.4 = (f32[2,1,768,4,64]{2,4,3,1,0:T(8,128)S(1)}, f32[2,1,768,4,64]{2,4,3,1,0:T(8,128)}, u32[]{:S(2)}) copy-start(f32[2,1,768,4,64]{2,4,3,1,0:T(8,128)} %get-tuple-element.117) | copy-start | bytes 4718596
  70.2 3.8 %copy-start.11 = (pred[8]{0:T(512)(128)(4,1)S(1)}, pred[8]{0:T(512)(128)(4,1)}, u32[]{:S(2)}) copy-start(pred[8]{0:T(512)(128)(4,1)} %get-tuple-element.187) | copy-start | bytes 28
  76.7 29.5 %all-to-all-start.1 = ((bf16[2,8,128,256]{3,2,0,1:T(8,128)(2,1)}), bf16[2,8,128,256]{3,2,0,1:T(8,128)(2,1)}, u32[]{:S(2)}, u32[]{:S(2)}) async-start(bf16[2,8,128,256]{3,2,0,1:T(8,128)(2,1)} %fusion.34), calls=%async_computation.1 | async-start | bytes 2097152 | tf_op jit(solution)/shard_map/all_to_all | solution.py:149
  80.9 40.9 %reduce-scatter.2.cloned.1.call-start = ((), (), s32[]{:S(2)}) async-start(), calls=%async_computation.3 | async-start | bytes 393216 | tf_op jit(solution)/shard_map/reduce_scatter | solution.py:166
  81.5 2.2 %copy-start.10 = (bf16[2,1,128,4,64]{2,4,3,1,0:T(8,128)(2,1)S(1)}, bf16[2,1,128,4,64]{2,4,3,1,0:T(8,128)(2,1)}, u32[]{:S(2)}) copy-start(bf16[2,1,128,4,64]{2,4,3,1,0:T(8,128)(2,1)} %copy-done.9) | copy-start | bytes 393220
  81.6 5.9 %collective-permute-start.2 = (bf16[2,1,128,256]{3,2,1,0:T(8,128)(2,1)S(1)}, bf16[2,1,128,256]{3,2,1,0:T(8,128)(2,1)S(1)}, u32[]{:S(2)}, u32[]{:S(2)}) collective-permute-start(bf16[2,1,128,256]{3,2,1,0:T(8,128)(2,1)S(1)} %slice.266), channel_id=1, source_target_pairs={{0,2},{2,0},{1,3},{3,1},{4,6},{6,4},{5,7},{7,5},{8,10},{10,8},{9,1... | collective-permute-start | bytes 393224 | tf_op jit(solution)/shard_map/ppermute | solution.py:25
  83.2 5.8 %collective-permute-start.3 = (bf16[2,1,128,256]{3,2,1,0:T(8,128)(2,1)S(1)}, bf16[2,1,128,256]{3,2,1,0:T(8,128)(2,1)S(1)}, u32[]{:S(2)}, u32[]{:S(2)}) collective-permute-start(bf16[2,1,128,256]{3,2,1,0:T(8,128)(2,1)S(1)} %slice.265), channel_id=1, source_target_pairs={{0,2},{2,0},{1,3},{3,1},{4,6},{6,4},{5,7},{7,5},{8,10},{10,8},{9,1... | collective-permute-start | bytes 393224 | tf_op jit(solution)/shard_map/ppermute | solution.py:25
  111.0 1.0 copy-start.6
  111.2 1.0 copy-start.8
Sparse Core Ops, SparseCore 0:
  115.0 6.7 reduce-scatter.1
where the time goes:
time: 129 us
  waiting for transfers between devices  48.8 us (38%)
  local copies, waits for them, and re-layouts  30.6 us (24%)
  starting transfers between devices  15.1 us (12%)
  between operations  13.9 us (11%)
  other arithmetic  10.2 us (8%)
  matrix products  9.91 us (8%)
    all_to_all x1, waiting for transfers between devices, body(): lax.all_to_all(sent_slots, 'slab', split_axis=1, concat_axis=1, tiled=True)  17.8 us
    all_to_all x1, waiting for transfers between devices, body(): lax.all_to_all(outgoing.astype(jnp.bfloat16), 'slab', split_axis=1, conca...  17.2 us
    another operation x4, local copies, waits for them, and re-layouts, body(): jnp.stack([grad_key, grad_value])  8.01 us
    reduce_scatter x1, waiting for transfers between devices, body(): lax.psum_scatter(placed.astype(jnp.bfloat16), 'head', scatter_dimension=1...  6.94 us
    all_to_all x1, starting transfers between devices, body(): lax.all_to_all(sent_slots, 'slab', split_axis=1, concat_axis=1, tiled=True)  6.45 us
    ppermute x2, waiting for transfers between devices, from_behind(): return lax.ppermute(value, axis, pairs)  4.81 us
    all_to_all x1, starting transfers between devices, body(): lax.all_to_all(outgoing.astype(jnp.bfloat16), 'slab', split_axis=1, conca...  4.25 us
    gather x2, local copies, waits for them, and re-layouts, body(): jnp.take(returned, item_slot, axis=1)  3.38 us
  transfers between devices with their start and end apart: 7, of which 7 were waited for; matrix products, arithmetic and copies ran while one was open for 4% of the time, Pallas kernels for 0%

commit v1 on v0

--- a/solution.py
+++ b/solution.py
@@ -146,9 +146,30 @@
     )
     padded = jnp.concatenate([far_terms, jnp.zeros_like(far_terms[:, :1])], axis=1)
     outgoing = jnp.take(padded, slot_item, axis=1)
-    returned = lax.all_to_all(
-        outgoing.astype(jnp.bfloat16), "slab", split_axis=1, concat_axis=1, tiled=True
-    ).astype(outgoing.dtype)
+
+    def draft_matrix(block_in, mesh_dim):
+        all_rows, state_now = (lax.axis_size(mesh_dim), lax.axis_index(mesh_dim))
+        answer = block_in.shape[1] // all_rows
+        p_next = list(block_in.shape)
+        p_next[1] = answer
+        t_next = p_next[1]
+        p_next[1] = t_next * all_rows
+        part_next = jnp.zeros(p_next, block_in.dtype)
+        for dev_i in range(all_rows):
+            response = lax.dynamic_slice_in_dim(
+                block_in, (state_now ^ dev_i) * answer, answer, axis=1
+            )
+            if dev_i:
+                in_order = []
+                for k in range(all_rows):
+                    in_order.append((k, k ^ dev_i))
+                response = lax.ppermute(response, mesh_dim, in_order)
+            part_next = lax.dynamic_update_slice_in_dim(
+                part_next, response, (state_now ^ dev_i) * t_next, axis=1
+            )
+        return part_next
+
+    returned = draft_matrix(outgoing.astype(jnp.bfloat16), "slab").astype(outgoing.dtype)
     returned_terms = jnp.take(returned, item_slot, axis=1).reshape(
         2, 3, block_count, block_len, feat_width
     )

time: 129 us -> 118 us (0.915)
  waiting for transfers between devices: 48.8 us -> 44.9 us
  other arithmetic: 10.2 us -> 6.8 us
  local copies, waits for them, and re-layouts: 30.6 us -> 28 us
    all_to_all x1 -> x0, waiting for transfers between devices: 17.2 us -> none  [body(): lax.all_to_all(outgoing.astype(jnp.bfloat16), 'slab', split_axis=1, conca...]
    ppermute x0 -> x3, waiting for transfers between devices: none -> 10.5 us  [draft_matrix(): response = lax.ppermute(response, mesh_dim, in_order)]
    ppermute x0 -> x3, starting transfers between devices: none -> 4.44 us  [draft_matrix(): response = lax.ppermute(response, mesh_dim, in_order)]
    all_to_all x1 -> x0, starting transfers between devices: 4.25 us -> none  [body(): lax.all_to_all(outgoing.astype(jnp.bfloat16), 'slab', split_axis=1, conca...]
    reduce_scatter x1, waiting for transfers between devices: 6.94 us -> 9.74 us  [body(): lax.psum_scatter(placed.astype(jnp.bfloat16), 'head', scatter_dimension=1...]
    convert_element_type x1, other arithmetic: 2.6 us -> 0.41 us  [body(): outgoing.astype(jnp.bfloat16)]
    gather x1, local copies, waits for them, and re-layouts: 2.75 us -> 0.61 us  [body(): outgoing = jnp.take(padded, slot_item, axis=1)]
  transfers between devices with their start and end apart: 7 -> 9, of which waited for: 7 -> 8; matrix products, arithmetic and copies ran while one was open for 4% -> 3% of each run, Pallas kernels for 0% -> 0%
where the time goes in v1:
time: 118 us
  waiting for transfers between devices  44.9 us (38%)
  local copies, waits for them, and re-layouts  28 us (24%)
  starting transfers between devices  15 us (13%)
  between operations  14 us (12%)
  matrix products  8.97 us (8%)
  other arithmetic  6.8 us (6%)
    all_to_all x1, waiting for transfers between devices, body(): lax.all_to_all(sent_slots, 'slab', split_axis=1, concat_axis=1, tiled=True)  17.8 us
    ppermute x3, waiting for transfers between devices, draft_matrix(): response = lax.ppermute(response, mesh_dim, in_order)  10.5 us
    reduce_scatter x1, waiting for transfers between devices, body(): lax.psum_scatter(placed.astype(jnp.bfloat16), 'head', scatter_dimension=1...  9.74 us
    another operation x4, local copies, waits for them, and re-layouts, body(): jnp.stack([grad_key, grad_value])  8 us
    all_to_all x1, starting transfers between devices, body(): lax.all_to_all(sent_slots, 'slab', split_axis=1, concat_axis=1, tiled=True)  6.45 us
    ppermute x3, starting transfers between devices, draft_matrix(): response = lax.ppermute(response, mesh_dim, in_order)  4.44 us
    ppermute x2, waiting for transfers between devices, from_behind(): return lax.ppermute(value, axis, pairs)  3.85 us
    gather x2, local copies, waits for them, and re-layouts, body(): jnp.take(returned, item_slot, axis=1)  3.4 us
  transfers between devices with their start and end apart: 9, of which 8 were waited for; matrix products, arithmetic and copies ran while one was open for 3% of the time, Pallas kernels for 0%

profile of v1, /device:TPU:0, one launch (start us, length us, event | category | flops | bytes accessed | tf_op | source)
XLA Modules:
  0.0 117.8 jit_solution(211933010456176238)
XLA Ops:
  6.5 0.7 compare_select_fusion.1
  8.0 0.8 copy.98
  9.7 2.2 %gather_fusion.4 = bf16[256,512]{1,0:T(8,128)(2,1)S(1)} fusion(bf16[256,512]{1,0:T(8,128)(2,1)} %param.23, s32[1024]{0:T(1024)S(1)} %pad_clamp_fusion.3), kind=kCustom, calls=%fused_computation.clone | custom fusion | bytes 525312 | tf_op jit(solution)/shard_map/jit(_take)/gather | solution.py:78
  13.2 1.1 select_bitcast_fusion
  14.4 6.5 %all-to-all-start = ((bf16[2,8,128,256]{3,2,0,1:T(8,128)(2,1)}), bf16[2,8,128,256]{3,2,0,1:T(8,128)(2,1)S(1)}, u32[]{:S(2)}, u32[]{:S(2)}) async-start(bf16[2,8,128,256]{3,2,0,1:T(8,128)(2,1)} %select_bitcast_fusion), calls=%async_computation | async-start | bytes 2097152 | tf_op jit(solution)/shard_map/all_to_all | solution.py:105
  20.9 1.6 %collective-permute-start = (bf16[2,128,256]{2,1,0:T(8,128)(2,1)S(1)}, bf16[2,128,256]{2,1,0:T(8,128)(2,1)S(1)}, u32[]{:S(2)}, u32[]{:S(2)}) collective-permute-start(bf16[2,128,256]{2,1,0:T(8,128)(2,1)S(1)} %get-tuple-element.198), channel_id=1, source_target_pairs={{0,2},{2,0},{1,3},{3,1},{4,6},{6,4},{5,7},{7,5},{8,10},{10,8},{9,1... | collective-permute-start | bytes 393224 | tf_op jit(solution)/shard_map/ppermute | solution.py:16
  23.1 1.2 gather_fusion.5
  25.7 1.6 %collective-permute-done = bf16[2,128,256]{2,1,0:T(8,128)(2,1)S(1)} collective-permute-done((bf16[2,128,256]{2,1,0:T(8,128)(2,1)S(1)}, bf16[2,128,256]{2,1,0:T(8,128)(2,1)S(1)}, u32[]{:S(2)}, u32[]{:S(2)}) %collective-permute-start) | collective-permute-done | bytes 131104 | tf_op jit(solution)/shard_map/ppermute | solution.py:16
  27.3 1.4 %collective-permute-done.1 = bf16[2,128,256]{2,1,0:T(8,128)(2,1)S(1)} collective-permute-done((bf16[2,128,256]{2,1,0:T(8,128)(2,1)S(1)}, bf16[2,128,256]{2,1,0:T(8,128)(2,1)S(1)}, u32[]{:S(2)}, u32[]{:S(2)}) %collective-permute-start.1) | collective-permute-done | bytes 131104 | tf_op jit(solution)/shard_map/ppermute | solution.py:17
  28.8 17.8 %all-to-all-done = bf16[2,8,128,256]{3,2,0,1:T(8,128)(2,1)S(1)} async-done(((bf16[2,8,128,256]{3,2,0,1:T(8,128)(2,1)}), bf16[2,8,128,256]{3,2,0,1:T(8,128)(2,1)S(1)}, u32[]{:S(2)}, u32[]{:S(2)}) %all-to-all-start) | async-done | bytes 1048608 | tf_op jit(solution)/shard_map/all_to_all | solution.py:105
  47.7 0.9 copy.105
  48.6 0.9 reshape_squeeze.6
  49.5 0.8 copy.108
  50.3 0.9 reshape_squeeze.7
  51.2 10.4 %while.19 = (s32[]{:T(128)}, bf16[2,1,128,4,64]{2,4,3,1,0:T(8,128)(2,1)S(1)}, f32[2,1,768,4,64]{2,4,3,1,0:T(8,128)}, f32[2,1,768,4,64]{2,4,3,1,0:T(8,128)}, bf16...) while((s32[]{:T(128)}, ...), condition=%wide.region_7.9_spmd, body=%wide.region_3.0_spmd.sunk | while | flops 307428352 | bytes 26441652 | solution.py:121
  54.8 1.2 fusion.104
  60.0 1.2 fusion.104
  61.5 2.7 %stack.40 = f32[1,2,6,128,256]{3,2,4,1,0:T(8,128)} reshape(f32[2,1,768,4,64]{2,4,3,1,0:T(8,128)} %get-tuple-element.116) | data formatting | bytes 3145728 | tf_op jit(solution)/shard_map/stack | solution.py:133
  64.2 1.9 %copy.115 = f32[1,2,6,128,256]{4,3,1,0,2:T(8,128)S(1)} copy(f32[1,2,6,128,256]{3,2,4,1,0:T(8,128)} %stack.40) | data formatting | bytes 3145728 | tf_op jit(solution)/shard_map/stack | solution.py:133
  66.2 1.6 %stack.41 = f32[1,2,6,128,256]{3,2,4,1,0:T(8,128)} reshape(f32[2,1,768,4,64]{2,4,3,1,0:T(8,128)S(1)} %copy-done.6) | data formatting | bytes 3145728 | tf_op jit(solution)/shard_map/stack | solution.py:133
  67.8 1.8 %copy.116 = f32[1,2,6,128,256]{4,3,1,0,2:T(8,128)S(1)} copy(f32[1,2,6,128,256]{3,2,4,1,0:T(8,128)} %stack.41) | data formatting | bytes 3145728 | tf_op jit(solution)/shard_map/stack | solution.py:133
  72.3 2.0 %collective-permute-start.5 = (bf16[2,2,128,256]{3,2,0,1:T(8,128)(2,1)S(1)}, bf16[2,2,128,256]{3,2,0,1:T(8,128)(2,1)S(1)}, u32[]{:S(2)}, u32[]{:S(2)}) collective-permute-start(bf16[2,2,128,256]{3,2,0,1:T(8,128)(2,1)S(1)} %get-tuple-element.190), channel_id=1, source_target_pairs={{0,8},{4,12},{8,0},{12,4},{1,9},{5,13},{9,1},{13,5},{2,10},{6,14},... | collective-permute-start | bytes 786440 | tf_op jit(solution)/shard_map/ppermute | solution.py:166
  74.3 2.4 %collective-permute-start.6 = (bf16[2,2,128,256]{3,2,0,1:T(8,128)(2,1)S(1)}, bf16[2,2,128,256]{3,2,0,1:T(8,128)(2,1)S(1)}, u32[]{:S(2)}, u32[]{:S(2)}) collective-permute-start(bf16[2,2,128,256]{3,2,0,1:T(8,128)(2,1)S(1)} %get-tuple-element.189), channel_id=1, source_target_pairs={{0,12},{4,8},{8,4},{12,0},{1,13},{5,9},{9,5},{13,1},{2,14},{6,10},... | collective-permute-start | bytes 786440 | tf_op jit(solution)/shard_map/ppermute | solution.py:166
  76.7 1.5 %collective-permute-start.2 = (bf16[2,1,128,256]{3,2,1,0:T(8,128)(2,1)S(1)}, bf16[2,1,128,256]{3,2,1,0:T(8,128)(2,1)S(1)}, u32[]{:S(2)}, u32[]{:S(2)}) collective-permute-start(bf16[2,1,128,256]{3,2,1,0:T(8,128)(2,1)S(1)} %slice.266), channel_id=1, source_target_pairs={{0,2},{2,0},{1,3},{3,1},{4,6},{6,4},{5,7},{7,5},{8,10},{10,8},{9,1... | collective-permute-start | bytes 393224 | tf_op jit(solution)/shard_map/ppermute | solution.py:25
  79.2 2.4 %collective-permute-done.2 = bf16[2,1,128,256]{3,2,1,0:T(8,128)(2,1)S(1)} collective-permute-done((bf16[2,1,128,256]{3,2,1,0:T(8,128)(2,1)S(1)}, bf16[2,1,128,256]{3,2,1,0:T(8,128)(2,1)S(1)}, u32[]{:S(2)}, u32[]{:S(2)}) %collective-permute-start.2) | collective-permute-done | bytes 131104 | tf_op jit(solution)/shard_map/ppermute | solution.py:25
  81.7 1.4 %collective-permute-done.3 = bf16[2,1,128,256]{3,2,1,0:T(8,128)(2,1)S(1)} collective-permute-done((bf16[2,1,128,256]{3,2,1,0:T(8,128)(2,1)S(1)}, bf16[2,1,128,256]{3,2,1,0:T(8,128)(2,1)S(1)}, u32[]{:S(2)}, u32[]{:S(2)}) %collective-permute-start.3) | collective-permute-done | bytes 131104 | tf_op jit(solution)/shard_map/ppermute | solution.py:25
  83.2 1.2 %collective-permute-done.4 = bf16[2,2,128,256]{3,2,0,1:T(8,128)(2,1)S(1)} collective-permute-done((bf16[2,2,128,256]{3,2,0,1:T(8,128)(2,1)S(1)}, bf16[2,2,128,256]{3,2,0,1:T(8,128)(2,1)S(1)}, u32[]{:S(2)}, u32[]{:S(2)}) %collective-permute-start.4) | collective-permute-done | bytes 262176 | tf_op jit(solution)/shard_map/ppermute | solution.py:166
  84.4 9.3 %collective-permute-done.5 = bf16[2,2,128,256]{3,2,0,1:T(8,128)(2,1)S(1)} collective-permute-done((bf16[2,2,128,256]{3,2,0,1:T(8,128)(2,1)S(1)}, bf16[2,2,128,256]{3,2,0,1:T(8,128)(2,1)S(1)}, u32[]{:S(2)}, u32[]{:S(2)}) %collective-permute-start.5) | collective-permute-done | bytes 262176 | tf_op jit(solution)/shard_map/ppermute | solution.py:166
  94.0 1.8 %gather_fusion.3 = f32[6,2,128,256]{3,2,1,0:T(8,128)} fusion(f32[2,8,128,256]{3,2,1,0:T(8,128)S(1)} %convert_element_type.78, s32[1024]{0:T(1024)S(1)} %pad_clamp_fusion.1), kind=kCustom, calls=%fused_computation.5 | custom fusion | bytes 3145752 | tf_op jit(solution)/shard_map/jit(_take)/gather | solution.py:173
  95.8 1.6 %copy.122 = f32[2,6,128,256]{3,2,1,0:T(8,128)S(1)} copy(f32[2,6,128,256]{3,2,0,1:T(8,128)} %bitcast.210) | data formatting | bytes 3145728 | tf_op jit(solution)/shard_map/jit(_take)/gather | solution.py:173
  98.9 1.6 %scatter_custom_fusion = f32[256,512]{1,0:T(8,128)S(1)} fusion(s32[256]{0:T(256)S(1)} %compare_select_fusion.1, f32[256,512]{1,0:T(8,128)S(1)} %convolution_add_fusion, f32[]{:T(128)} %constant.258.clone.1), kind=kCustom, calls=%fused_computation.94 | custom fusion | bytes 524292 | tf_op jit(solution)/shard_map/scatter | solution.py:186
  101.2 9.7 %reduce-scatter.2.cloned.1.call-done = bf16[256,256]{1,0:T(8,128)(2,1)} async-done(((bf16[256,512]{1,0:T(8,128)(2,1)}), bf16[256,256]{1,0:T(8,128)(2,1)}) %reduce-scatter.2.cloned.1.call-update) | async-done | bytes 131088 | tf_op jit(solution)/shard_map/reduce_scatter | solution.py:187
  (124 shorter events, 20.1 us)
Async XLA Ops:
  6.5 17.8 %copy-start = (bf16[512,256]{1,0:T(8,128)(2,1)S(1)}, bf16[512,256]{1,0:T(8,128)(2,1)}, u32[]{:S(2)}) copy-start(bf16[512,256]{1,0:T(8,128)(2,1)} %param.25) | copy-start | bytes 786436
  6.5 5.5 %copy-start.7 = (bf16[512,256]{1,0:T(8,128)(2,1)S(1)}, bf16[512,256]{1,0:T(8,128)(2,1)}, u32[]{:S(2)}) copy-start(bf16[512,256]{1,0:T(8,128)(2,1)} %param.26) | copy-start | bytes 786436
  9.7 2.5 %copy-start.9 = (bf16[512,256]{1,0:T(8,128)(2,1)S(1)}, bf16[512,256]{1,0:T(8,128)(2,1)}, u32[]{:S(2)}) copy-start(bf16[512,256]{1,0:T(8,128)(2,1)} %param.27) | copy-start | bytes 786436
  14.4 8.7 %copy-start.1 = (bf16[256,512]{1,0:T(8,128)(2,1)S(1)}, bf16[256,512]{1,0:T(8,128)(2,1)}, u32[]{:S(2)}) copy-start(bf16[256,512]{1,0:T(8,128)(2,1)} %param.24) | copy-start | bytes 786436
  14.4 32.2 %all-to-all-start = ((bf16[2,8,128,256]{3,2,0,1:T(8,128)(2,1)}), bf16[2,8,128,256]{3,2,0,1:T(8,128)(2,1)S(1)}, u32[]{:S(2)}, u32[]{:S(2)}) async-start(bf16[2,8,128,256]{3,2,0,1:T(8,128)(2,1)} %select_bitcast_fusion), calls=%async_computation | async-start | bytes 2097152 | tf_op jit(solution)/shard_map/all_to_all | solution.py:105
  20.8 3.5 %copy-start.13 = (s32[2,3]{1,0:T(2,128)S(1)}, s32[2,3]{1,0:T(2,128)}, u32[]{:S(2)}) copy-start(s32[2,3]{1,0:T(2,128)} %param.29) | copy-start | bytes 76
  20.8 90.1 %reduce-scatter.2.cloned.1.call-start = ((), (), s32[]{:S(2)}) async-start(), calls=%async_computation.2 | async-start | bytes 393216 | tf_op jit(solution)/shard_map/reduce_scatter | solution.py:187
  20.9 6.4 %collective-permute-start = (bf16[2,128,256]{2,1,0:T(8,128)(2,1)S(1)}, bf16[2,128,256]{2,1,0:T(8,128)(2,1)S(1)}, u32[]{:S(2)}, u32[]{:S(2)}) collective-permute-start(bf16[2,128,256]{2,1,0:T(8,128)(2,1)S(1)} %get-tuple-element.198), channel_id=1, source_target_pairs={{0,2},{2,0},{1,3},{3,1},{4,6},{6,4},{5,7},{7,5},{8,10},{10,8},{9,1... | collective-permute-start | bytes 393224 | tf_op jit(solution)/shard_map/ppermute | solution.py:16
  22.4 6.3 %collective-permute-start.1 = (bf16[2,128,256]{2,1,0:T(8,128)(2,1)S(1)}, bf16[2,128,256]{2,1,0:T(8,128)(2,1)S(1)}, u32[]{:S(2)}, u32[]{:S(2)}) collective-permute-start(bf16[2,128,256]{2,1,0:T(8,128)(2,1)S(1)} %get-tuple-element.199), channel_id=1, source_target_pairs={{2,0},{0,2},{3,1},{1,3},{6,4},{4,6},{7,5},{5,7},{10,8},{8,10},{11,... | collective-permute-start | bytes 393224 | tf_op jit(solution)/shard_map/ppermute | solution.py:17
  23.1 1.5 %copy-start.12 = (bf16[256,512]{1,0:T(8,128)(2,1)S(1)}, bf16[256,512]{1,0:T(8,128)(2,1)}, u32[]{:S(2)}) copy-start(bf16[256,512]{1,0:T(8,128)(2,1)} %param.28) | copy-start | bytes 786436
  51.3 1.4 %copy-start.4 = (f32[2,1,768,4,64]{2,4,3,1,0:T(8,128)S(1)}, f32[2,1,768,4,64]{2,4,3,1,0:T(8,128)}, u32[]{:S(2)}) copy-start(f32[2,1,768,4,64]{2,4,3,1,0:T(8,128)} %get-tuple-element.278) | copy-start | bytes 4718596 | tf_op jit(solution)/shard_map/while
  53.1 1.2 copy-start.5
  56.5 1.4 %copy-start.4 = (f32[2,1,768,4,64]{2,4,3,1,0:T(8,128)S(1)}, f32[2,1,768,4,64]{2,4,3,1,0:T(8,128)}, u32[]{:S(2)}) copy-start(f32[2,1,768,4,64]{2,4,3,1,0:T(8,128)} %get-tuple-element.278) | copy-start | bytes 4718596 | tf_op jit(solution)/shard_map/while
  58.3 1.2 copy-start.5
  64.2 2.0 %copy-start.6 = (f32[2,1,768,4,64]{2,4,3,1,0:T(8,128)S(1)}, f32[2,1,768,4,64]{2,4,3,1,0:T(8,128)}, u32[]{:S(2)}) copy-start(f32[2,1,768,4,64]{2,4,3,1,0:T(8,128)} %get-tuple-element.117) | copy-start | bytes 4718596
  70.1 0.8 copy-start.2
  71.0 0.7 copy-start.11
  72.2 9.5 %copy-start.3 = (f32[2,2,128,256]{3,2,1,0:T(8,128)S(1)}, f32[2,2,128,256]{3,2,1,0:T(8,128)}, u32[]{:S(2)}) copy-start(f32[2,2,128,256]{3,2,1,0:T(8,128)} %copy-done.2) | copy-start | bytes 1572868
  72.2 12.2 %collective-permute-start.4 = (bf16[2,2,128,256]{3,2,0,1:T(8,128)(2,1)S(1)}, bf16[2,2,128,256]{3,2,0,1:T(8,128)(2,1)S(1)}, u32[]{:S(2)}, u32[]{:S(2)}) collective-permute-start(bf16[2,2,128,256]{3,2,0,1:T(8,128)(2,1)S(1)} %get-tuple-element.191), channel_id=1, source_target_pairs={{0,4},{4,0},{8,12},{12,8},{1,5},{5,1},{9,13},{13,9},{2,6},{6,2},{1... | collective-permute-start | bytes 786440 | tf_op jit(solution)/shard_map/ppermute | solution.py:166
  72.3 21.4 %collective-permute-start.5 = (bf16[2,2,128,256]{3,2,0,1:T(8,128)(2,1)S(1)}, bf16[2,2,128,256]{3,2,0,1:T(8,128)(2,1)S(1)}, u32[]{:S(2)}, u32[]{:S(2)}) collective-permute-start(bf16[2,2,128,256]{3,2,0,1:T(8,128)(2,1)S(1)} %get-tuple-element.190), channel_id=1, source_target_pairs={{0,8},{4,12},{8,0},{12,4},{1,9},{5,13},{9,1},{13,5},{2,10},{6,14},... | collective-permute-start | bytes 786440 | tf_op jit(solution)/shard_map/ppermute | solution.py:166
  74.3 19.4 %collective-permute-start.6 = (bf16[2,2,128,256]{3,2,0,1:T(8,128)(2,1)S(1)}, bf16[2,2,128,256]{3,2,0,1:T(8,128)(2,1)S(1)}, u32[]{:S(2)}, u32[]{:S(2)}) collective-permute-start(bf16[2,2,128,256]{3,2,0,1:T(8,128)(2,1)S(1)} %get-tuple-element.189), channel_id=1, source_target_pairs={{0,12},{4,8},{8,4},{12,0},{1,13},{5,9},{9,5},{13,1},{2,14},{6,10},... | collective-permute-start | bytes 786440 | tf_op jit(solution)/shard_map/ppermute | solution.py:166
  76.7 5.0 %collective-permute-start.2 = (bf16[2,1,128,256]{3,2,1,0:T(8,128)(2,1)S(1)}, bf16[2,1,128,256]{3,2,1,0:T(8,128)(2,1)S(1)}, u32[]{:S(2)}, u32[]{:S(2)}) collective-permute-start(bf16[2,1,128,256]{3,2,1,0:T(8,128)(2,1)S(1)} %slice.266), channel_id=1, source_target_pairs={{0,2},{2,0},{1,3},{3,1},{4,6},{6,4},{5,7},{7,5},{8,10},{10,8},{9,1... | collective-permute-start | bytes 393224 | tf_op jit(solution)/shard_map/ppermute | solution.py:25
  78.1 5.0 %collective-permute-start.3 = (bf16[2,1,128,256]{3,2,1,0:T(8,128)(2,1)S(1)}, bf16[2,1,128,256]{3,2,1,0:T(8,128)(2,1)S(1)}, u32[]{:S(2)}, u32[]{:S(2)}) collective-permute-start(bf16[2,1,128,256]{3,2,1,0:T(8,128)(2,1)S(1)} %slice.265), channel_id=1, source_target_pairs={{0,2},{2,0},{1,3},{3,1},{4,6},{6,4},{5,7},{7,5},{8,10},{10,8},{9,1... | collective-permute-start | bytes 393224 | tf_op jit(solution)/shard_map/ppermute | solution.py:25
  97.4 1.0 copy-start.8
  97.6 1.0 copy-start.10
Sparse Core Ops, SparseCore 0:
  101.3 9.5 reduce-scatter.1
